TPU v7x, 32 devices: a whole 2x2x4 slice. The times are simulated.
32 devices in a mesh: sub: 4 (over z), grp: 8 (over y, x, core).
Axes of the slice: x: 2, y: 2, z: 4, core: 2. Of those that a mesh axis runs over, the one named last changes fastest.
Arguments:
- schur: bfloat16 [128, 1024, 1024], P(('sub', 'grp')), as said below
- mortar: bfloat16 [128, 8, 128, 128], P(('sub', 'grp')), may hold values from -0.5 to 0.5
- partner: int32 [128, 4], P(('sub', 'grp')), may hold values from 0 to 15, as said below
- corner_map: int32 [128, 8], P(('sub', 'grp')), may hold values from 0 to 127
- coarse_inv: float32 [4, 128, 128], P('sub'), as said below
- load: float32 [128, 1024, 384], P(('sub', 'grp')), may hold values from -6 to 6
Outputs:
- solution: float32 [128, 1024, 384], P(('sub', 'grp'))
Inputs may be any that keep to these rules, and one draw needn't show every extreme that they name: `partner`: within the 4 subdomains of one device, the entries form a permutation of 0 to 15. `schur`: each matrix is symmetric positive definite. `coarse_inv`: each matrix is symmetric positive definite.
All inputs are finite; a program needn't handle non-finite values.
Results may differ from a plain program's by a relative error of at most 0.0025.
Values may be sent and summed in bfloat16 or wider, within the bound.
No kernel may reach another device: no remote copies, remote signals or barrier semaphores. Data moves between devices by JAX's collectives and lax.ppermute only.
A program may use at most 128 MiB of HBM per device.

v0:
```python
import jax
import jax.numpy as jnp
from jax import lax
from jax.sharding import PartitionSpec as P

ITERS = 2


def shifted(block, axis, distance):
    devices = range(lax.axis_size(axis))
    route = [((i - distance) % len(devices), i) for i in devices]
    return lax.ppermute(block, axis, route)


def face_terms(direction, schur, mortar, partner):
    subdoms = direction.shape[0]
    order = direction.shape[1]
    columns = direction.shape[2]
    faces_all = mortar.shape[1]
    block = mortar.shape[2]
    half_faces = faces_all // 2
    dir_half = direction.astype(jnp.bfloat16)
    stiff = jnp.einsum("sij,sjr->sir", schur, dir_half, preferred_element_type=jnp.float32)
    face_rows = dir_half.reshape(subdoms, faces_all, block, columns)
    traces = jnp.einsum(
        "sfij,sfjr->sfir", mortar, face_rows, preferred_element_type=jnp.float32
    ).astype(jnp.bfloat16)
    upper = traces[:, :half_faces].reshape(subdoms * half_faces, block, columns)
    lower = traces[:, half_faces:].reshape(subdoms * half_faces, block, columns)
    mates = partner.reshape(-1)
    inverse = jnp.argsort(mates)
    reordered = jnp.take(upper, inverse, axis=0)
    lower_mate = shifted(reordered, "sub", 1)
    jump_lower = (lower.astype(jnp.float32) - lower_mate.astype(jnp.float32)).astype(jnp.bfloat16)
    above = shifted(lower, "sub", -1)
    upper_mate = jnp.take(above, mates, axis=0)
    jump_upper = (upper.astype(jnp.float32) - upper_mate.astype(jnp.float32)).astype(jnp.bfloat16)
    jump_all = jnp.concatenate(
        [
            jump_upper.reshape(subdoms, half_faces, block, columns),
            jump_lower.reshape(subdoms, half_faces, block, columns),
        ],
        axis=1,
    )
    pulled = jnp.einsum("sfji,sfjr->sfir", mortar, jump_all, preferred_element_type=jnp.float32)
    return stiff + pulled.reshape(subdoms, order, columns)


def squares(residual):
    return lax.psum(jnp.sum(residual * residual, axis=(0, 1)), ("sub", "grp"))


def on_device(schur, mortar, partner, corner_map, coarse_inv, load):
    order = load.shape[1]
    corner_count = corner_map.shape[1]
    coarse_count = coarse_inv.shape[1]
    stride = order // corner_count
    onehot = (corner_map[..., None] == jnp.arange(coarse_count, dtype=jnp.int32)).astype(
        jnp.float32
    )
    coarse_matrix = coarse_inv[0]
    solution = jnp.zeros_like(load)
    residual = load
    direction = load
    norm_now = squares(residual)
    for step in range(ITERS):
        partial_value = face_terms(direction, schur, mortar, partner)
        corners = direction[:, ::stride, :]
        local_sum = jnp.einsum("sco,scr->or", onehot, corners, precision=lax.Precision.HIGHEST)
        local_dot = jnp.sum(direction * partial_value, axis=(0, 1))
        coarse_sum = lax.psum(local_sum.astype(jnp.bfloat16), "grp").astype(jnp.float32)
        group_dot = lax.psum(local_dot.astype(jnp.bfloat16), "grp").astype(jnp.float32)
        coarse_val = jnp.dot(coarse_matrix, coarse_sum, precision=lax.Precision.HIGHEST)
        corner_add = jnp.einsum("sco,or->scr", onehot, coarse_val, precision=lax.Precision.HIGHEST)
        image = partial_value.at[:, ::stride, :].add(corner_add)
        curvature = lax.psum(group_dot + jnp.sum(coarse_sum * coarse_val, axis=0), "sub")
        image, curvature = (image, curvature)
        step_len = norm_now / curvature
        solution = solution + step_len * direction
        if step + 1 < ITERS:
            residual = residual - step_len * image
            norm_next = squares(residual)
            direction = residual + norm_next / norm_now * direction
            norm_now = norm_next
    return solution


def solution(mesh):
    return jax.shard_map(
        on_device,
        mesh=mesh,
        in_specs=(
            P(("sub", "grp"), None, None),
            P(("sub", "grp"), None, None, None),
            P(("sub", "grp"), None),
            P(("sub", "grp"), None),
            P("sub", None, None),
            P(("sub", "grp"), None, None),
        ),
        out_specs=P(("sub", "grp"), None, None),
        check_vma=False,
    )
```

profile of v0, /device:TPU:0, one launch (start us, length us, event | category | flops | bytes accessed | tf_op | source)
XLA Modules:
  0.0 398.2 jit_solution(7781319759656753900)
XLA Ops:
  6.5 0.0 all-reduce.3.cloned.1.call-start
  6.5 3.2 convert_element_type.76
  9.8 1.0 convolution_convert_fusion
  10.8 0.0 copy-start.3
  10.8 1.5 fusion.33
  12.3 5.1 %collective-permute-start = (bf16[16,128,384]{2,1,0:T(8,128)(2,1)}, bf16[16,128,384]{2,1,0:T(8,128)(2,1)}, u32[]{:S(2)}, u32[]{:S(2)}) collective-permute-start(bf16[16,128,384]{2,1,0:T(8,128)(2,1)} %bitcast.2), channel_id=1, source_target_pairs={{8,0},{16,8},{24,16},{0,24},{9,1},{17,9},{25,17},{1,25},{10,2},{18... | collective-permute-start | bytes 4718600 | tf_op jit(solution)/shard_map/ppermute | solution.py:12
  17.4 0.1 reshape.59
  17.5 1.2 sort.19
  18.8 0.0 copy-start.2
  18.8 1.9 gather_fusion.1
  20.7 2.8 broadcast_select_fusion.1
  23.5 0.0 collective-permute-start.1
  23.5 2.8 slice.20
  26.3 1.0 fusion.17
  27.3 0.0 all-reduce.3.cloned.1.call-update
  27.3 0.0 all-reduce.5.cloned.1.call-start
  27.4 0.0 copy-start.1
  27.4 6.6 %copy.8 = f32[4,1024,384]{1,2,0:T(8,128)} copy(f32[4,1024,384]{2,1,0:T(8,128)} %param.13) | data formatting | bytes 12582912 | tf_op args[5]
  34.0 46.9 %all-reduce.3.cloned.1.call-done = bf16[128,384]{1,0:T(8,128)(2,1)} async-done(((bf16[128,384]{1,0:T(8,128)(2,1)}), bf16[128,384]{1,0:T(8,128)(2,1)}) %all-reduce.3.cloned.1.call-update) | async-done | bytes 98320 | tf_op jit(solution)/shard_map/psum | solution.py:71
  81.0 1.2 fusion.21
  82.2 0.2 convolution_bitcast_fusion.3
  82.4 0.0 collective-permute-done
  82.4 3.3 gather_fusion
  85.8 2.1 subtract_convert_fusion.3
  87.9 0.0 collective-permute-done.1
  87.9 0.0 slice-start
  87.9 2.5 subtract_convert_fusion.2
  90.4 0.0 slice-start.1
  90.4 3.7 fusion.5
  94.1 12.9 %multiply_reduce_fusion.1 = (bf16[384]{0:T(512)(128)(2,1)S(1)}, f32[384]{0:T(512)S(1)}, f32[4,1024,384]{2,1,0:T(8,128)}) fusion(f32[4,1024,384]{2,1,0:T(8,128)S(1)} %bitcast.79, f32[4,8,384,128]{2,3,1,0:T(8,128)} %fusion.5, bf16[4,1024,1024]{2,1,0:T(8,128)(2,1)} %param.8), kind=kOutput, calls=%fused_computation.13 | convolution fusion | flops 3230661632 | bytes 27265280 | tf_op jit(solution)/shard_map/sij,sjr->sir/dot_general | solution.py:23
  107.0 12.8 %psum.57 = bf16[384]{0:T(512)(128)(2,1)S(1)} all-reduce(bf16[384]{0:T(512)(128)(2,1)S(1)} %get-tuple-element.8), channel_id=1, replica_groups=mesh['sub'=4,'grp'=8] {'grp'}, use_global_device_ids=true, to_apply=%region_4.6 | all-reduce | flops 384 | bytes 1536 | tf_op jit(solution)/shard_map/psum | solution.py:72
  119.8 11.7 %psum.59 = f32[384]{0:T(512)S(1)} all-reduce(f32[384]{0:T(512)S(1)} %convert_add_fusion.1), channel_id=1, replica_groups=mesh['sub'=4,'grp'=8] {'sub'}, use_global_device_ids=true, to_apply=%region_7.9 | all-reduce | flops 384 | bytes 3072 | tf_op jit(solution)/shard_map/psum | solution.py:76
  131.5 37.0 %psum.56 = f32[384]{0:T(512)S(1)} all-reduce(f32[384]{0:T(512)S(1)} %get-tuple-element.9), channel_id=1, replica_groups=mesh['sub'=4,'grp'=8] {'sub','grp'}, use_global_device_ids=true, to_apply=%region_1.0 | all-reduce | flops 384 | bytes 3072 | tf_op jit(solution)/shard_map/psum | solution.py:50
  168.5 9.5 %copy.10 = f32[4,1024,384]{2,0,1:T(4,128)} copy(f32[4,1024,384]{2,1,0:T(8,128)} %get-tuple-element.16) | data formatting | bytes 12582912 | tf_op jit(solution)/shard_map/add | solution.py:46
  178.0 2.1 scatter_fusion
  180.0 7.6 %copy.12 = f32[4,1024,384]{1,2,0:T(8,128)} copy(f32[4,1024,384]{2,0,1:T(4,128)} %scatter_fusion) | data formatting | bytes 12582912 | tf_op jit(solution)/shard_map/scatter-add | solution.py:75
  187.7 5.6 %multiply_reduce_fusion = f32[384]{0:T(512)S(1)} fusion(f32[4,1024,384]{1,2,0:T(8,128)} %copy.8, f32[4,1024,384]{1,2,0:T(8,128)} %copy.12, f32[384]{0:T(512)S(1)} %div.9), kind=kLoop, calls=%fused_computation.11 | loop fusion | flops 6291072 | bytes 12585984 | tf_op jit(solution)/shard_map/reduce_sum | solution.py:50
  193.3 42.2 %psum.60 = f32[384]{0:T(512)S(1)} all-reduce(f32[384]{0:T(512)S(1)} %multiply_reduce_fusion), channel_id=1, replica_groups=mesh['sub'=4,'grp'=8] {'sub','grp'}, use_global_device_ids=true, to_apply=%region_10.12 | all-reduce | flops 384 | bytes 3072 | tf_op jit(solution)/shard_map/psum | solution.py:50
  235.5 7.7 %convert_bitcast_fusion.1 = (bf16[4,48,8,8,128]{4,3,2,1,0:T(8,128)(2,1)S(1)}, f32[4,1024,384]{1,2,0:T(8,128)}) fusion(f32[4,1024,384]{1,2,0:T(8,128)} %copy.8, f32[384]{0:T(512)S(1)} %div.10, f32[4,1024,384]{1,2,0:T(8,128)} %copy.12, f32[384]{0:T(512)S(1)} %div.9), kind=kLoop, calls=%fused_computation.32 | loop fusion | flops 7864320 | bytes 22023168
  243.2 1.0 convert_bitcast_fusion
  244.2 1.4 fusion.32
  245.6 1.6 collective-permute-start.2
  247.1 1.9 gather_fusion.3
  249.0 2.8 broadcast_select_fusion
  251.8 0.5 collective-permute-start.3
  252.3 4.3 %slice.23 = f32[4,8,384]{1,2,0:T(8,128)S(1)} slice(f32[4,1024,384]{1,2,0:T(8,128)} %get-tuple-element.11), slice={[0:4:1], [0:1024:128], [0:384:1]} | slice | bytes 98304 | tf_op jit(solution)/shard_map/slice | solution.py:68
  256.6 1.2 fusion.18
  257.9 0.0 all-reduce.5.cloned.1.call-update
  257.9 53.1 %all-reduce.5.cloned.1.call-done = bf16[128,384]{1,0:T(8,128)(2,1)} async-done(((bf16[128,384]{1,0:T(8,128)(2,1)}), bf16[128,384]{1,0:T(8,128)(2,1)}) %all-reduce.5.cloned.1.call-update) | async-done | bytes 98320 | tf_op jit(solution)/shard_map/psum | solution.py:71
  310.9 1.2 fusion.19
  312.1 2.8 collective-permute-done.2
  314.9 3.3 gather_fusion.2
  318.3 3.2 subtract_convert_fusion.1
  321.4 1.9 copy.16
  323.3 0.0 collective-permute-done.3
  323.3 3.4 subtract_convert_fusion
  326.8 2.6 copy.17
  329.3 5.1 %fusion.9 = f32[4,8,384,128]{2,3,1,0:T(8,128)} fusion(bf16[4,8,128,128]{3,2,1,0:T(8,128)(2,1)S(1)} %copy-done, bf16[4,4,128,384]{3,2,1,0:T(8,128)(2,1)} %bitcast.87, bf16[4,4,128,384]{3,2,1,0:T(8,128)(2,1)S(1)} %bitcast.85), kind=kOutput, calls=%fused_computation.22 | convolution fusion | flops 404226048 | bytes 10485760 | tf_op jit(solution)/shard_map/sfji,sfjr->sfir/dot_general | solution.py:45
  334.4 6.5 %copy.27 = f32[4,1024,384]{1,2,0:T(8,128)} copy(f32[4,1024,384]{2,1,0:T(8,128)} %bitcast.80) | data formatting | bytes 12582912 | tf_op jit(solution)/shard_map/reshape | solution.py:46
  340.9 12.5 %fusion.1 = bf16[384]{0:T(512)(128)(2,1)S(1)} fusion(f32[4,1024,384]{1,2,0:T(8,128)} %get-tuple-element.11, f32[4,1024,384]{1,2,0:T(8,128)} %copy.27, bf16[4,1024,1024]{2,1,0:T(8,128)(2,1)} %param.8), kind=kOutput, calls=%fused_computation.8 | convolution fusion | flops 3227516416 | bytes 20972288 | tf_op jit(solution)/shard_map/sij,sjr->sir/dot_general | solution.py:23
  353.5 11.8 %psum.61 = bf16[384]{0:T(512)(128)(2,1)S(1)} all-reduce(bf16[384]{0:T(512)(128)(2,1)S(1)} %fusion.1), channel_id=1, replica_groups=mesh['sub'=4,'grp'=8] {'grp'}, use_global_device_ids=true, to_apply=%region_12.14 | all-reduce | flops 384 | bytes 1536 | tf_op jit(solution)/shard_map/psum | solution.py:72
  365.3 9.9 %psum.63 = f32[384]{0:T(512)S(1)} all-reduce(f32[384]{0:T(512)S(1)} %convert_add_fusion), channel_id=1, replica_groups=mesh['sub'=4,'grp'=8] {'sub'}, use_global_device_ids=true, to_apply=%region_15.17 | all-reduce | flops 384 | bytes 3072 | tf_op jit(solution)/shard_map/psum | solution.py:76
  375.2 9.6 %multiply_add_fusion = f32[4,1024,384]{1,2,0:T(8,128)} fusion(f32[4,1024,384]{1,2,0:T(8,128)} %get-tuple-element.11, f32[4,1024,384]{1,2,0:T(8,128)} %copy.8, f32[384]{0:T(512)S(1)} %div.11, f32[384]{0:T(512)S(1)} %div.9), kind=kLoop, calls=%fused_computation.9 | loop fusion | flops 4718592 | bytes 18877440 | tf_op jit(solution)/shard_map/add | solution.py:79
  384.8 6.6 %copy.21 = f32[4,1024,384]{2,1,0:T(8,128)} copy(f32[4,1024,384]{1,2,0:T(8,128)} %multiply_add_fusion) | data formatting | bytes 12582912 | tf_op jit(solution)/shard_map/add | solution.py:79
  (22 shorter events, 0.1 us)
Async XLA Ops:
  6.5 3.2 copy-start
  6.5 74.4 %all-reduce.3.cloned.1.call-start = ((), (), s32[]{:S(2)}) async-start(), calls=%async_computation | async-start | bytes 196608 | tf_op jit(solution)/shard_map/psum | solution.py:71
  10.8 6.6 %copy-start.3 = (s32[4,4]{1,0:T(4,128)S(1)}, s32[4,4]{1,0:T(4,128)}, u32[]{:S(2)}) copy-start(s32[4,4]{1,0:T(4,128)} %param.10) | copy-start | bytes 196
  12.3 70.1 %collective-permute-start = (bf16[16,128,384]{2,1,0:T(8,128)(2,1)}, bf16[16,128,384]{2,1,0:T(8,128)(2,1)}, u32[]{:S(2)}, u32[]{:S(2)}) collective-permute-start(bf16[16,128,384]{2,1,0:T(8,128)(2,1)} %bitcast.2), channel_id=1, source_target_pairs={{8,0},{16,8},{24,16},{0,24},{9,1},{17,9},{25,17},{1,25},{10,2},{18... | collective-permute-start | bytes 4718600 | tf_op jit(solution)/shard_map/ppermute | solution.py:12
  18.8 7.5 %copy-start.2 = (s32[4,8]{1,0:T(4,128)S(1)}, s32[4,8]{1,0:T(4,128)}, u32[]{:S(2)}) copy-start(s32[4,8]{1,0:T(4,128)} %param.11) | copy-start | bytes 388
  23.5 64.4 %collective-permute-start.1 = (bf16[16,128,384]{2,1,0:T(8,128)(2,1)}, bf16[16,128,384]{2,1,0:T(8,128)(2,1)}, u32[]{:S(2)}, u32[]{:S(2)}) collective-permute-start(bf16[16,128,384]{2,1,0:T(8,128)(2,1)} %broadcast_select_fusion.1), channel_id=1, source_target_pairs={{24,0},{0,8},{8,16},{16,24},{25,1},{1,9},{9,17},{17,25},{26,2},{2,... | collective-permute-start | bytes 4718600 | tf_op jit(solution)/shard_map/ppermute | solution.py:12
  27.3 283.6 %all-reduce.5.cloned.1.call-start = ((), (), s32[]{:S(2)}) async-start(), calls=%async_computation.1 | async-start | bytes 196608 | tf_op jit(solution)/shard_map/psum | solution.py:71
  27.4 53.5 %copy-start.1 = (f32[1,128,128]{2,1,0:T(8,128)S(1)}, f32[1,128,128]{2,1,0:T(8,128)}, u32[]{:S(2)}) copy-start(f32[1,128,128]{2,1,0:T(8,128)} %param.12) | copy-start | bytes 196612
  87.9 6.2 %slice-start = ((s8[6291456]{0:T(1024)(128)(4,1)}), s8[4194304]{0:T(1024)(128)(4,1)S(1)}, s32[]{:S(2)}) async-start(s8[6291456]{0:T(1024)(128)(4,1)} %bitcast.78), calls=%async_computation.2 | async-start | bytes 8388608
  90.4 3.7 slice-start.1
  245.6 69.3 %collective-permute-start.2 = (bf16[16,128,384]{1,2,0:T(8,128)(2,1)}, bf16[16,128,384]{1,2,0:T(8,128)(2,1)}, u32[]{:S(2)}, u32[]{:S(2)}) collective-permute-start(bf16[16,128,384]{1,2,0:T(8,128)(2,1)} %bitcast.16), channel_id=1, source_target_pairs={{8,0},{16,8},{24,16},{0,24},{9,1},{17,9},{25,17},{1,25},{10,2},{18... | collective-permute-start | bytes 4718600 | tf_op jit(solution)/shard_map/ppermute | solution.py:12
  251.8 71.5 %collective-permute-start.3 = (bf16[16,128,384]{1,2,0:T(8,128)(2,1)}, bf16[16,128,384]{1,2,0:T(8,128)(2,1)}, u32[]{:S(2)}, u32[]{:S(2)}) collective-permute-start(bf16[16,128,384]{1,2,0:T(8,128)(2,1)} %broadcast_select_fusion), channel_id=1, source_target_pairs={{24,0},{0,8},{8,16},{16,24},{25,1},{1,9},{9,17},{17,25},{26,2},{2,... | collective-permute-start | bytes 4718600 | tf_op jit(solution)/shard_map/ppermute | solution.py:12
Sparse Core Ops, SparseCore 0:
  27.4 53.4 all-reduce.2
  258.0 52.8 all-reduce.4
where the time goes:
time: 399 us; the launch traced here: 398 us
  blocking collectives  125 us (31%)
  waiting for transfers between devices  103 us (26%)
  local copies, waits for them, and re-layouts  61.9 us (16%)
  other arithmetic  46.2 us (12%)
  matrix products  41.1 us (10%)
  between operations  13.6 us (3%)
  starting transfers between devices  7.15 us (2%)
    psum x2, waiting for transfers between devices, on_device(): lax.psum(local_sum.astype(jnp.bfloat16), 'grp').astype(jnp.float32)  100 us
    psum x2, blocking collectives, squares(): return lax.psum(jnp.sum(residual * residual, axis=(0, 1)), ('sub', 'grp'))  79.2 us
    dot_general x2, matrix products, face_terms(): jnp.einsum('sij,sjr->sir', schur, dir_half, preferred_element_type=jnp.fl...  25.4 us
    psum x2, blocking collectives, on_device(): lax.psum(local_dot.astype(jnp.bfloat16), 'grp').astype(jnp.float32)  24.6 us
    psum x2, blocking collectives, on_device(): lax.psum(group_dot + jnp.sum(coarse_sum * coarse_val, axis=0), 'sub')  21.6 us
    add x1, other arithmetic, on_device(): solution = solution + step_len * direction  9.61 us
    add x1, local copies, waits for them, and re-layouts, face_terms(): return stiff + pulled.reshape(subdoms, order, columns)  9.48 us
    dot_general x2, matrix products, face_terms(): jnp.einsum('sfji,sfjr->sfir', mortar, jump_all, preferred_element_type=jn...  8.78 us
  transfers between devices with their start and end apart: 6, of which 3 were waited for; matrix products, arithmetic and copies ran while one was open for 11% of the time, Pallas kernels for 0%

commit v1 on v0

--- a/solution.py
+++ b/solution.py
@@ -4,6 +4,11 @@
 from jax.sharding import PartitionSpec as P
 
 ITERS = 2
+
+
+def get_files(own_rows):
+    side_arr = jax.lax.all_gather(own_rows, ("sub", "grp")).sum(axis=0)
+    return side_arr
 
 
 def shifted(block, axis, distance):
@@ -47,7 +52,7 @@
 
 
 def squares(residual):
-    return lax.psum(jnp.sum(residual * residual, axis=(0, 1)), ("sub", "grp"))
+    return get_files(jnp.sum(residual * residual, axis=(0, 1)))
 
 
 def on_device(schur, mortar, partner, corner_map, coarse_inv, load):

time: 399 us -> 395 us (0.990)
  blocking collectives: 125 us -> 120 us
    psum x2 -> x0, blocking collectives: 79.2 us -> none  [squares(): return lax.psum(jnp.sum(residual * residual, axis=(0, 1)), ('sub', 'grp'))]
    all_gather x0 -> x2, blocking collectives: none -> 75.1 us  [get_files(): side_arr = jax.lax.all_gather(own_rows, ('sub', 'grp')).sum(axis=0)]
    ppermute x4, waiting for transfers between devices: 2.79 us -> 7.37 us  [shifted(): return lax.ppermute(block, axis, route)]
where the time goes in v1:
time: 395 us; the launch traced here: 394 us
  blocking collectives  120 us (30%)
  waiting for transfers between devices  104 us (26%)
  local copies, waits for them, and re-layouts  61.9 us (16%)
  other arithmetic  46.4 us (12%)
  matrix products  41.1 us (10%)
  between operations  13.6 us (3%)
  starting transfers between devices  7.15 us (2%)
    psum x2, waiting for transfers between devices, on_device(): lax.psum(local_sum.astype(jnp.bfloat16), 'grp').astype(jnp.float32)  96.7 us
    all_gather x2, blocking collectives, get_files(): side_arr = jax.lax.all_gather(own_rows, ('sub', 'grp')).sum(axis=0)  75.1 us
    dot_general x2, matrix products, face_terms(): jnp.einsum('sij,sjr->sir', schur, dir_half, preferred_element_type=jnp.fl...  25.4 us
    psum x2, blocking collectives, on_device(): lax.psum(local_dot.astype(jnp.bfloat16), 'grp').astype(jnp.float32)  24.6 us
    psum x2, blocking collectives, on_device(): lax.psum(group_dot + jnp.sum(coarse_sum * coarse_val, axis=0), 'sub')  20 us
    add x1, other arithmetic, on_device(): solution = solution + step_len * direction  9.61 us
    add x1, local copies, waits for them, and re-layouts, face_terms(): return stiff + pulled.reshape(subdoms, order, columns)  9.48 us
    dot_general x2, matrix products, face_terms(): jnp.einsum('sfji,sfjr->sfir', mortar, jump_all, preferred_element_type=jn...  8.78 us
  transfers between devices with their start and end apart: 6, of which 3 were waited for; matrix products, arithmetic and copies ran while one was open for 11% of the time, Pallas kernels for 0%

profile of v1, /device:TPU:0, one launch (start us, length us, event | category | flops | bytes accessed | tf_op | source)
XLA Modules:
  0.0 394.0 jit_solution(4392535690592030623)
XLA Ops:
  6.5 3.2 convert_element_type.76
  9.8 1.0 convolution_convert_fusion
  10.8 0.0 copy-start.3
  10.8 1.5 fusion.33
  12.3 5.1 %collective-permute-start = (bf16[16,128,384]{2,1,0:T(8,128)(2,1)}, bf16[16,128,384]{2,1,0:T(8,128)(2,1)}, u32[]{:S(2)}, u32[]{:S(2)}) collective-permute-start(bf16[16,128,384]{2,1,0:T(8,128)(2,1)} %bitcast.2), channel_id=1, source_target_pairs={{8,0},{16,8},{24,16},{0,24},{9,1},{17,9},{25,17},{1,25},{10,2},{18... | collective-permute-start | bytes 4718600 | tf_op jit(solution)/shard_map/ppermute | solution.py:17
  17.4 0.1 reshape.63
  17.5 1.2 sort.19
  18.8 0.0 copy-start.2
  18.8 1.9 gather_fusion.1
  20.7 2.8 broadcast_select_fusion.1
  23.5 0.0 collective-permute-start.1
  23.5 2.8 slice.20
  26.3 1.0 fusion.17
  27.3 0.0 all-reduce.3.cloned.1.call-update
  27.3 0.0 all-reduce.5.cloned.1.call-start
  27.4 0.0 copy-start.1
  27.4 6.6 %copy.23 = f32[4,1024,384]{1,2,0:T(8,128)} copy(f32[4,1024,384]{2,1,0:T(8,128)} %param.13) | data formatting | bytes 12582912 | tf_op args[5]
  34.0 46.9 %all-reduce.3.cloned.1.call-done = bf16[128,384]{1,0:T(8,128)(2,1)} async-done(((bf16[128,384]{1,0:T(8,128)(2,1)}), bf16[128,384]{1,0:T(8,128)(2,1)}) %all-reduce.3.cloned.1.call-update) | async-done | bytes 98320 | tf_op jit(solution)/shard_map/psum | solution.py:76
  81.0 1.2 fusion.21
  82.2 0.2 convolution_bitcast_fusion.3
  82.4 3.3 gather_fusion
  85.8 2.1 subtract_convert_fusion.3
  87.9 0.0 collective-permute-done.1
  87.9 0.0 slice-start
  87.9 2.5 subtract_convert_fusion.2
  90.4 0.0 slice-start.1
  90.4 3.7 fusion.5
  94.1 12.9 %multiply_reduce_fusion.1 = (bf16[384]{0:T(512)(128)(2,1)S(1)}, f32[384]{0:T(512)S(1)}, f32[4,1024,384]{2,1,0:T(8,128)}) fusion(f32[4,1024,384]{2,1,0:T(8,128)S(1)} %bitcast.79, f32[4,8,384,128]{2,3,1,0:T(8,128)} %fusion.5, bf16[4,1024,1024]{2,1,0:T(8,128)(2,1)} %param.8), kind=kOutput, calls=%fused_computation.13 | convolution fusion | flops 3230661632 | bytes 27265280 | tf_op jit(solution)/shard_map/sij,sjr->sir/dot_general | solution.py:28
  107.0 12.8 %psum.42 = bf16[384]{0:T(512)(128)(2,1)S(1)} all-reduce(bf16[384]{0:T(512)(128)(2,1)S(1)} %get-tuple-element.8), channel_id=1, replica_groups=mesh['sub'=4,'grp'=8] {'grp'}, use_global_device_ids=true, to_apply=%region_4.6 | all-reduce | flops 384 | bytes 1536 | tf_op jit(solution)/shard_map/psum | solution.py:77
  119.8 11.7 %psum.44 = f32[384]{0:T(512)S(1)} all-reduce(f32[384]{0:T(512)S(1)} %convert_add_fusion.1), channel_id=1, replica_groups=mesh['sub'=4,'grp'=8] {'sub'}, use_global_device_ids=true, to_apply=%region_7.9 | all-reduce | flops 384 | bytes 3072 | tf_op jit(solution)/shard_map/psum | solution.py:81
  131.5 36.6 %all-gather.2 = f32[32,1,384]{2,1,0:T(1,128)S(1)} all-gather(f32[1,1,384]{2,1,0:T(1,128)S(1)} %reshape.119), channel_id=2, replica_groups=mesh['sub'=4,'grp'=8] {'sub','grp'}, dimensions={0}, use_global_device_ids=true | all-gather | bytes 50688 | tf_op jit(solution)/shard_map/all_gather | solution.py:10
  168.1 9.5 %copy.25 = f32[4,1024,384]{2,0,1:T(4,128)} copy(f32[4,1024,384]{2,1,0:T(8,128)} %get-tuple-element.16) | data formatting | bytes 12582912 | tf_op jit(solution)/shard_map/add | solution.py:51
  177.6 2.1 scatter_fusion
  179.7 7.6 %copy.27 = f32[4,1024,384]{1,2,0:T(8,128)} copy(f32[4,1024,384]{2,0,1:T(4,128)} %scatter_fusion) | data formatting | bytes 12582912 | tf_op jit(solution)/shard_map/scatter-add | solution.py:80
  187.3 0.1 reduce_sum.73
  187.4 5.6 %multiply_reduce_fusion = f32[384]{0:T(512)S(1)} fusion(f32[4,1024,384]{1,2,0:T(8,128)} %copy.23, f32[4,1024,384]{1,2,0:T(8,128)} %copy.27, f32[384]{0:T(512)S(1)} %div.13), kind=kLoop, calls=%fused_computation.11 | loop fusion | flops 6291072 | bytes 12585984 | tf_op jit(solution)/shard_map/reduce_sum | solution.py:55
  193.0 38.4 %all-gather.3 = f32[32,1,384]{2,1,0:T(1,128)S(1)} all-gather(f32[1,1,384]{2,1,0:T(1,128)S(1)} %reshape.121), channel_id=3, replica_groups=mesh['sub'=4,'grp'=8] {'sub','grp'}, dimensions={0}, use_global_device_ids=true | all-gather | bytes 50688 | tf_op jit(solution)/shard_map/all_gather | solution.py:10
  231.4 0.1 reduce_sum.77
  231.5 7.7 %convert_bitcast_fusion.1 = (bf16[4,48,8,8,128]{4,3,2,1,0:T(8,128)(2,1)S(1)}, f32[4,1024,384]{1,2,0:T(8,128)}) fusion(f32[4,1024,384]{1,2,0:T(8,128)} %copy.23, f32[384]{0:T(512)S(1)} %div.14, f32[4,1024,384]{1,2,0:T(8,128)} %copy.27, f32[384]{0:T(512)S(1)} %div.13), kind=kLoop, calls=%fused_computation.32 | loop fusion | flops 7864320 | bytes 22023168
  239.2 1.0 convert_bitcast_fusion
  240.1 1.4 fusion.32
  241.6 0.0 collective-permute-start.2
  241.6 1.9 gather_fusion.3
  243.5 2.8 broadcast_select_fusion
  246.2 2.0 collective-permute-start.3
  248.3 4.3 %slice.23 = f32[4,8,384]{1,2,0:T(8,128)S(1)} slice(f32[4,1024,384]{1,2,0:T(8,128)} %get-tuple-element.11), slice={[0:4:1], [0:1024:128], [0:384:1]} | slice | bytes 98304 | tf_op jit(solution)/shard_map/slice | solution.py:73
  252.6 1.2 fusion.18
  253.8 0.0 all-reduce.5.cloned.1.call-update
  253.9 49.8 %all-reduce.5.cloned.1.call-done = bf16[128,384]{1,0:T(8,128)(2,1)} async-done(((bf16[128,384]{1,0:T(8,128)(2,1)}), bf16[128,384]{1,0:T(8,128)(2,1)}) %all-reduce.5.cloned.1.call-update) | async-done | bytes 98320 | tf_op jit(solution)/shard_map/psum | solution.py:76
  303.7 1.2 fusion.19
  304.9 7.4 %collective-permute-done.2 = bf16[16,128,384]{1,2,0:T(8,128)(2,1)} collective-permute-done((bf16[16,128,384]{1,2,0:T(8,128)(2,1)}, bf16[16,128,384]{1,2,0:T(8,128)(2,1)}, u32[]{:S(2)}, u32[]{:S(2)}) %collective-permute-start.2) | collective-permute-done | bytes 1572896 | tf_op jit(solution)/shard_map/ppermute | solution.py:17
  312.3 3.3 gather_fusion.2
  315.6 3.2 subtract_convert_fusion.1
  318.8 1.9 copy.31
  320.6 0.0 collective-permute-done.3
  320.6 3.4 subtract_convert_fusion
  324.1 2.6 copy.32
  326.6 5.1 %fusion.9 = f32[4,8,384,128]{2,3,1,0:T(8,128)} fusion(bf16[4,8,128,128]{3,2,1,0:T(8,128)(2,1)S(1)} %copy-done, bf16[4,4,128,384]{3,2,1,0:T(8,128)(2,1)} %bitcast.87, bf16[4,4,128,384]{3,2,1,0:T(8,128)(2,1)S(1)} %bitcast.85), kind=kOutput, calls=%fused_computation.22 | convolution fusion | flops 404226048 | bytes 10485760 | tf_op jit(solution)/shard_map/sfji,sfjr->sfir/dot_general | solution.py:50
  331.7 6.5 %copy.42 = f32[4,1024,384]{1,2,0:T(8,128)} copy(f32[4,1024,384]{2,1,0:T(8,128)} %bitcast.80) | data formatting | bytes 12582912 | tf_op jit(solution)/shard_map/reshape | solution.py:51
  338.3 12.5 %fusion.1 = bf16[384]{0:T(512)(128)(2,1)S(1)} fusion(f32[4,1024,384]{1,2,0:T(8,128)} %get-tuple-element.11, f32[4,1024,384]{1,2,0:T(8,128)} %copy.42, bf16[4,1024,1024]{2,1,0:T(8,128)(2,1)} %param.8), kind=kOutput, calls=%fused_computation.8 | convolution fusion | flops 3227516416 | bytes 20972288 | tf_op jit(solution)/shard_map/sij,sjr->sir/dot_general | solution.py:28
  350.8 11.8 %psum.45 = bf16[384]{0:T(512)(128)(2,1)S(1)} all-reduce(bf16[384]{0:T(512)(128)(2,1)S(1)} %fusion.1), channel_id=1, replica_groups=mesh['sub'=4,'grp'=8] {'grp'}, use_global_device_ids=true, to_apply=%region_12.14 | all-reduce | flops 384 | bytes 1536 | tf_op jit(solution)/shard_map/psum | solution.py:77
  362.6 8.4 %psum.47 = f32[384]{0:T(512)S(1)} all-reduce(f32[384]{0:T(512)S(1)} %convert_add_fusion), channel_id=1, replica_groups=mesh['sub'=4,'grp'=8] {'sub'}, use_global_device_ids=true, to_apply=%region_15.17 | all-reduce | flops 384 | bytes 3072 | tf_op jit(solution)/shard_map/psum | solution.py:81
  371.0 9.6 %multiply_add_fusion = f32[4,1024,384]{1,2,0:T(8,128)} fusion(f32[4,1024,384]{1,2,0:T(8,128)} %get-tuple-element.11, f32[4,1024,384]{1,2,0:T(8,128)} %copy.23, f32[384]{0:T(512)S(1)} %div.15, f32[384]{0:T(512)S(1)} %div.13), kind=kLoop, calls=%fused_computation.9 | loop fusion | flops 4718592 | bytes 18877440 | tf_op jit(solution)/shard_map/add | solution.py:84
  380.6 6.6 %copy.36 = f32[4,1024,384]{2,1,0:T(8,128)} copy(f32[4,1024,384]{1,2,0:T(8,128)} %multiply_add_fusion) | data formatting | bytes 12582912 | tf_op jit(solution)/shard_map/add | solution.py:84
  (26 shorter events, 0.1 us)
Async XLA Ops:
  6.5 3.2 copy-start
  6.5 74.4 %all-reduce.3.cloned.1.call-start = ((), (), s32[]{:S(2)}) async-start(), calls=%async_computation | async-start | bytes 196608 | tf_op jit(solution)/shard_map/psum | solution.py:76
  10.8 6.6 %copy-start.3 = (s32[4,4]{1,0:T(4,128)S(1)}, s32[4,4]{1,0:T(4,128)}, u32[]{:S(2)}) copy-start(s32[4,4]{1,0:T(4,128)} %param.10) | copy-start | bytes 196
  12.3 70.1 %collective-permute-start = (bf16[16,128,384]{2,1,0:T(8,128)(2,1)}, bf16[16,128,384]{2,1,0:T(8,128)(2,1)}, u32[]{:S(2)}, u32[]{:S(2)}) collective-permute-start(bf16[16,128,384]{2,1,0:T(8,128)(2,1)} %bitcast.2), channel_id=1, source_target_pairs={{8,0},{16,8},{24,16},{0,24},{9,1},{17,9},{25,17},{1,25},{10,2},{18... | collective-permute-start | bytes 4718600 | tf_op jit(solution)/shard_map/ppermute | solution.py:17
  18.8 7.5 %copy-start.2 = (s32[4,8]{1,0:T(4,128)S(1)}, s32[4,8]{1,0:T(4,128)}, u32[]{:S(2)}) copy-start(s32[4,8]{1,0:T(4,128)} %param.11) | copy-start | bytes 388
  23.5 64.4 %collective-permute-start.1 = (bf16[16,128,384]{2,1,0:T(8,128)(2,1)}, bf16[16,128,384]{2,1,0:T(8,128)(2,1)}, u32[]{:S(2)}, u32[]{:S(2)}) collective-permute-start(bf16[16,128,384]{2,1,0:T(8,128)(2,1)} %broadcast_select_fusion.1), channel_id=1, source_target_pairs={{24,0},{0,8},{8,16},{16,24},{25,1},{1,9},{9,17},{17,25},{26,2},{2,... | collective-permute-start | bytes 4718600 | tf_op jit(solution)/shard_map/ppermute | solution.py:17
  27.3 276.3 %all-reduce.5.cloned.1.call-start = ((), (), s32[]{:S(2)}) async-start(), calls=%async_computation.1 | async-start | bytes 196608 | tf_op jit(solution)/shard_map/psum | solution.py:76
  27.4 53.5 %copy-start.1 = (f32[1,128,128]{2,1,0:T(8,128)S(1)}, f32[1,128,128]{2,1,0:T(8,128)}, u32[]{:S(2)}) copy-start(f32[1,128,128]{2,1,0:T(8,128)} %param.12) | copy-start | bytes 196612
  87.9 6.2 %slice-start = ((s8[6291456]{0:T(1024)(128)(4,1)}), s8[4194304]{0:T(1024)(128)(4,1)S(1)}, s32[]{:S(2)}) async-start(s8[6291456]{0:T(1024)(128)(4,1)} %bitcast.78), calls=%async_computation.2 | async-start | bytes 8388608
  90.4 3.7 slice-start.1
  241.6 70.7 %collective-permute-start.2 = (bf16[16,128,384]{1,2,0:T(8,128)(2,1)}, bf16[16,128,384]{1,2,0:T(8,128)(2,1)}, u32[]{:S(2)}, u32[]{:S(2)}) collective-permute-start(bf16[16,128,384]{1,2,0:T(8,128)(2,1)} %bitcast.16), channel_id=1, source_target_pairs={{8,0},{16,8},{24,16},{0,24},{9,1},{17,9},{25,17},{1,25},{10,2},{18... | collective-permute-start | bytes 4718600 | tf_op jit(solution)/shard_map/ppermute | solution.py:17
  246.2 74.4 %collective-permute-start.3 = (bf16[16,128,384]{1,2,0:T(8,128)(2,1)}, bf16[16,128,384]{1,2,0:T(8,128)(2,1)}, u32[]{:S(2)}, u32[]{:S(2)}) collective-permute-start(bf16[16,128,384]{1,2,0:T(8,128)(2,1)} %broadcast_select_fusion), channel_id=1, source_target_pairs={{24,0},{0,8},{8,16},{16,24},{25,1},{1,9},{9,17},{17,25},{26,2},{2,... | collective-permute-start | bytes 4718600 | tf_op jit(solution)/shard_map/ppermute | solution.py:17
Sparse Core Ops, SparseCore 0:
  27.4 53.4 all-reduce.2
  254.0 49.6 all-reduce.4
